TPU v7x, 32 devices: a whole 2x2x4 slice. The times are simulated.
32 devices in a mesh: layer: 2 (over core), feat: 8 (over z, x), dp: 2 (over y).
Axes of the slice: x: 2, y: 2, z: 4, core: 2. Of those that a mesh axis runs over, the one named last changes fastest.
Arguments:
- resid: bfloat16 [2, 256, 1792], P('layer', 'dp', 'feat'), may hold values from -6 to 6
- target: bfloat16 [2, 256, 1792], P('layer', 'feat', 'dp'), may hold values from -6 to 6
- enc_weight: bfloat16 [2, 1792, 4096], P('layer', None, 'feat'), may hold values from -6 to 6
- enc_bias: float32 [2, 4096], P('layer', 'feat'), may hold values from -3 to 3
- dec_weight: bfloat16 [2, 2, 4096, 1792], P('layer', None, 'feat', 'dp'), may hold values from -6 to 6
- dec_bias: float32 [2, 1792], P('layer', 'dp'), may hold values from -3 to 3
Outputs:
- new_enc_weight: bfloat16 [2, 1792, 4096], P('layer', 'dp', 'feat')
- new_enc_bias: float32 [2, 4096], P('layer', 'feat')
- new_dec_weight: bfloat16 [2, 2, 4096, 1792], P('layer', None, 'feat', 'dp')
- new_dec_bias: float32 [2, 1792], P('layer', 'dp')
All inputs are finite; a program needn't handle non-finite values.
Results may differ from a plain program's by a relative error of at most 0.0065.
Values may be sent and summed in bfloat16 or wider, within the bound.
No kernel may reach another device: no remote copies, remote signals or barrier semaphores. Data moves between devices by JAX's collectives and lax.ppermute only.
A program may use at most 64 MiB of HBM per device.

v0:
```python
import jax
import jax.numpy as jnp
from jax import lax
from jax.sharding import PartitionSpec as P

step_weight = 256.0
step_bias = 4.0


def contract_rows(left, right):
    return lax.dot_general(
        left, right, (((0,), (0,)), ((), ())), preferred_element_type=jnp.float32
    )


def contract_width(left, right):
    return lax.dot_general(
        left, right, (((1,), (1,)), ((), ())), preferred_element_type=jnp.float32
    )


def local(resid, target, enc_weight, enc_bias, dec_weight, dec_bias):
    layer_count = lax.axis_size("layer")
    layer_index = lax.axis_index("layer")
    width = enc_weight.shape[1]
    feat_dev = enc_weight.shape[2]
    half_width = dec_weight.shape[3]
    enc_scale = width ** (-0.5)
    dec_scale = (feat_dev * lax.axis_size("feat")) ** (-0.5)
    inputs = lax.all_gather(resid[0], "feat", axis=1, tiled=True)
    preact = (
        enc_scale * jnp.dot(inputs, enc_weight[0], preferred_element_type=jnp.float32) + enc_bias[0]
    )
    codes = jnp.maximum(preact, 0.0).astype(jnp.bfloat16)
    token_codes = lax.all_gather(codes, "dp", axis=0, tiled=True)
    row_count = token_codes.shape[0]
    all_codes = lax.all_gather(token_codes[:, None, :], "layer", axis=1, tiled=True)
    scale_rows = dec_scale / row_count
    blocks = dec_weight[0]
    sources = jnp.arange(layer_count)
    alive = sources <= layer_index
    masked_codes = jnp.where(alive[None, :, None], all_codes, jnp.zeros((), jnp.bfloat16)).reshape(
        row_count, layer_count * feat_dev
    )
    flat_blocks = blocks.reshape(layer_count * feat_dev, half_width)
    picked = masked_codes
    summed = lax.psum_scatter(
        dec_scale * jnp.dot(picked, flat_blocks, preferred_element_type=jnp.float32),
        "feat",
        scatter_dimension=0,
        tiled=True,
    )
    recon = summed + dec_bias[0]
    local_errors = (recon - target[0].astype(jnp.float32)).astype(jnp.bfloat16)
    errors = lax.all_gather(local_errors, "feat", axis=0, tiled=True)
    dec_grad = (scale_rows * contract_rows(masked_codes, errors)).reshape(
        layer_count, feat_dev, half_width
    )
    new_blocks = (blocks.astype(jnp.float32) - step_weight * dec_grad).astype(jnp.bfloat16)
    new_dec_bias = dec_bias[0] - step_bias * jnp.sum(errors.astype(jnp.float32), axis=0) / row_count
    picked = errors
    terms = scale_rows * contract_width(picked, flat_blocks).reshape(
        row_count, layer_count, feat_dev
    )
    by_layer = lax.psum_scatter(
        terms * alive[None, :, None].astype(jnp.float32), "layer", scatter_dimension=1, tiled=True
    )
    code_grad = lax.psum_scatter(by_layer, "dp", scatter_dimension=0, tiled=True)[:, 0, :]
    pre_grad = jnp.where(preact > 0.0, code_grad, jnp.zeros_like(code_grad)).astype(jnp.bfloat16)
    enc_grad = enc_scale * contract_rows(inputs, pre_grad)
    bias_grad = jnp.sum(pre_grad.astype(jnp.float32), axis=0)
    dp_count = lax.axis_size("dp")
    dp_index = lax.axis_index("dp")
    share = width // dp_count
    enc_part, bias_rows = (
        lax.psum_scatter(enc_grad, "dp", scatter_dimension=0, tiled=True),
        lax.psum_scatter(
            jnp.broadcast_to(bias_grad[None, :], (dp_count, feat_dev)),
            "dp",
            scatter_dimension=0,
            tiled=True,
        ),
    )
    bias_total = bias_rows[0]
    old_part = lax.dynamic_slice_in_dim(enc_weight[0], dp_index * share, share, 0)
    new_enc = (old_part.astype(jnp.float32) - step_weight * enc_part).astype(jnp.bfloat16)
    new_enc_bias = enc_bias[0] - step_bias * bias_total
    return (new_enc[None], new_enc_bias[None], new_blocks[None], new_dec_bias[None])


def solution(mesh):
    placed = (
        P("layer", "dp", "feat"),
        P("layer", "feat", "dp"),
        P("layer", None, "feat"),
        P("layer", "feat"),
        P("layer", None, "feat", "dp"),
        P("layer", "dp"),
    )
    return jax.shard_map(
        local,
        mesh=mesh,
        in_specs=placed,
        out_specs=(
            P("layer", "dp", "feat"),
            P("layer", "feat"),
            P("layer", None, "feat", "dp"),
            P("layer", "dp"),
        ),
        check_vma=False,
    )
```

profile of v0, /device:TPU:0, one launch (start us, length us, event | category | flops | bytes accessed | tf_op | source)
XLA Modules:
  0.0 243.7 jit_solution(12601490794352313145)
XLA Ops:
  7.2 33.2 %all-gather = bf16[1,128,1792]{1,2,0:T(8,128)(2,1)S(1)} all-gather(bf16[1,128,224]{1,2,0:T(8,128)(2,1)} %param.6), channel_id=2, replica_groups=mesh['layer'=2,'feat'=8,'dp'=2] {'feat'}, dimensions={2}, use_global_device_ids=true | all-gather | bytes 516096 | tf_op jit(solution)/shard_map/all_gather | solution.py:30
  40.5 1.8 maximum_convert_fusion
  42.3 5.6 %all_gather.13 = bf16[256,512]{1,0:T(8,128)(2,1)S(1)} all-gather(bf16[128,512]{1,0:T(8,128)(2,1)S(1)} %get-tuple-element.14), channel_id=1, replica_groups=mesh['layer'=2,'feat'=8,'dp'=2] {'dp'}, dimensions={0}, use_global_device_ids=true | all-gather | bytes 393216 | tf_op jit(solution)/shard_map/all_gather | solution.py:35
  47.9 2.2 all-gather.1
  50.1 0.4 reshape.54
  50.5 0.5 broadcast_select_fusion
  51.0 0.1 copy.15
  51.1 0.9 copy-done.1
  52.0 1.6 convolution_multiply_fusion.1
  53.6 0.0 reduce-scatter.7.cloned.1.call-start
  53.7 64.8 %reduce-scatter.5.cloned.1.call-done = f32[32,896]{1,0:T(8,128)} async-done(((f32[256,896]{1,0:T(8,128)}), f32[32,896]{1,0:T(8,128)}) %reduce-scatter.5.cloned.1.call-update) | async-done | bytes 114704 | tf_op jit(solution)/shard_map/reduce_scatter | solution.py:47
  118.6 0.9 fusion.19
  119.5 31.3 %all_gather.15 = bf16[256,896]{1,0:T(8,128)(2,1)S(1)} all-gather(bf16[32,896]{1,0:T(8,128)(2,1)S(1)} %fusion.19), channel_id=1, replica_groups=mesh['layer'=2,'feat'=8,'dp'=2] {'feat'}, dimensions={0}, use_global_device_ids=true | all-gather | bytes 516096 | tf_op jit(solution)/shard_map/all_gather | solution.py:55
  150.8 3.3 %fusion.5 = f32[256,2,512]{2,0,1:T(8,128)} fusion(bf16[1,2,512,896]{3,2,1,0:T(8,128)(2,1)} %param.10, f32[2]{0:T(128)S(1)} %broadcast_select_fusion.1, bf16[256,896]{1,0:T(8,128)(2,1)S(1)} %all_gather.15), kind=kOutput, calls=%fused_computation.9 | convolution fusion | flops 470024192 | bytes 3342344 | tf_op jit(solution)/shard_map/dot_general | solution.py:17
  154.1 0.0 reduce-scatter.9.cloned.1.call-start
  154.1 7.2 %reduce-scatter.7.cloned.1.call-done = f32[256,1,512]{2,0,1:T(8,128)} async-done(((f32[256,2,512]{2,0,1:T(8,128)}), f32[256,1,512]{2,0,1:T(8,128)}) %reduce-scatter.7.cloned.1.call-update) | async-done | bytes 524304 | tf_op jit(solution)/shard_map/reduce_scatter | solution.py:65
  161.4 18.1 %reduce-scatter.9.cloned.1.call-done = f32[128,1,512]{2,0,1:T(8,128)} async-done(((f32[256,1,512]{2,0,1:T(8,128)}), f32[128,1,512]{2,0,1:T(8,128)}) %reduce-scatter.9.cloned.1.call-update) | async-done | bytes 262160 | tf_op jit(solution)/shard_map/reduce_scatter | solution.py:68
  179.4 1.0 convert_reduce_fusion.1
  180.5 2.5 %multiply_bitcast_fusion = f32[1792,512]{0,1:T(8,128)} fusion(bf16[128,512]{1,0:T(8,128)(2,1)S(1)} %get-tuple-element.13, bf16[1,128,1792]{1,2,0:T(8,128)(2,1)S(1)} %all-gather), kind=kOutput, calls=%fused_computation.1 | convolution fusion | flops 235798528 | bytes 4259840 | tf_op jit(solution)/shard_map/dot_general | solution.py:11
  183.0 1.0 constant_dynamic-slice_fusion
  184.0 2.2 copy.14
  186.2 0.6 dynamic-slice.1
  186.7 0.1 convert_reduce_fusion
  186.8 0.6 reshape_subtract_fusion
  187.4 0.7 convolution_multiply_fusion
  188.2 0.8 copy-done.2
  189.0 1.6 subtract_convert_fusion
  190.5 5.1 %all-reduce = f32[2,512]{1,0:T(2,128)S(1)} all-reduce(f32[2,512]{1,0:T(2,128)S(1)} %broadcast_in_dim.33), channel_id=8, replica_groups=mesh['layer'=2,'feat'=8,'dp'=2] {'dp'}, use_global_device_ids=true, to_apply=%region_5.6.clone | all-reduce | flops 1024 | bytes 8192
  195.7 1.2 fusion.20
  196.9 35.5 %reduce-scatter.11.cloned.1.call-done = f32[896,512]{0,1:T(8,128)} async-done(((f32[1792,512]{0,1:T(8,128)}), f32[896,512]{0,1:T(8,128)}) %reduce-scatter.11.cloned.1.call-update) | async-done | bytes 1835024 | tf_op jit(solution)/shard_map/reduce_scatter | solution.py:76
  232.4 2.6 %fusion.14 = bf16[1,896,512]{1,2,0:T(8,128)(2,1)} fusion(f32[896,512]{0,1:T(8,128)} %reduce-scatter.11.cloned.1.call-done, bf16[1,896,512]{1,2,0:T(8,128)(2,1)S(1)} %copy-done.3), kind=kLoop, calls=%fused_computation.14 | loop fusion | flops 1835008 | bytes 3670016 | tf_op jit(solution)/shard_map/broadcast_in_dim | solution.py:88
  235.0 2.2 copy.13
  (27 shorter events, 0.2 us)
Async XLA Ops:
  7.2 33.3 %copy-start = (bf16[1,1792,512]{2,1,0:T(8,128)(2,1)S(1)}, bf16[1,1792,512]{2,1,0:T(8,128)(2,1)}, u32[]{:S(2)}) copy-start(bf16[1,1792,512]{2,1,0:T(8,128)(2,1)} %param.8) | copy-start | bytes 5505028
  7.2 111.4 %reduce-scatter.5.cloned.1.call-start = ((), (), s32[]{:S(2)}) async-start(), calls=%async_computation.4 | async-start | bytes 1032192 | tf_op jit(solution)/shard_map/reduce_scatter | solution.py:47
  50.5 1.5 copy-start.1
  52.0 1.7 copy-start.6
  52.0 66.6 %copy-start.5 = (bf16[1,32,896]{2,1,0:T(8,128)(2,1)S(1)}, bf16[1,32,896]{2,1,0:T(8,128)(2,1)}, u32[]{:S(2)}) copy-start(bf16[1,32,896]{2,1,0:T(8,128)(2,1)} %param.7) | copy-start | bytes 172036
  53.6 107.7 %reduce-scatter.7.cloned.1.call-start = ((), (), s32[]{:S(2)}) async-start(), calls=%async_computation.5 | async-start | bytes 1572864 | tf_op jit(solution)/shard_map/reduce_scatter | solution.py:65
  150.8 28.6 %copy-start.4 = (f32[128,512]{1,0:T(8,128)S(1)}, f32[128,512]{1,0:T(8,128)}, u32[]{:S(2)}) copy-start(f32[128,512]{1,0:T(8,128)} %get-tuple-element.15) | copy-start | bytes 786436
  154.1 25.4 %reduce-scatter.9.cloned.1.call-start = ((), (), s32[]{:S(2)}) async-start(), calls=%async_computation.6 | async-start | bytes 786432 | tf_op jit(solution)/shard_map/reduce_scatter | solution.py:68
  161.3 71.0 %reduce-scatter.11.cloned.1.call-start = ((), (), s32[]{:S(2)}) async-start(), calls=%async_computation.7 | async-start | bytes 5505024 | tf_op jit(solution)/shard_map/reduce_scatter | solution.py:76
  183.0 3.2 %copy-start.8 = (u32[32]{0:T(128)S(1)}, u32[32]{0:T(128)}, u32[]{:S(2)}) copy-start(u32[32]{0:T(128)} %constant.47) | copy-start | bytes 388
  187.4 1.5 copy-start.2
  189.0 6.7 %copy-start.7 = (f32[1,512]{1,0:T(1,128)S(1)}, f32[1,512]{1,0:T(1,128)}, u32[]{:S(2)}) copy-start(f32[1,512]{1,0:T(1,128)} %param.9) | copy-start | bytes 6148
  189.0 43.4 %copy-start.3 = (bf16[1,896,512]{1,2,0:T(8,128)(2,1)S(1)}, bf16[1,896,512]{1,2,0:T(8,128)(2,1)}, u32[]{:S(2)}) copy-start(bf16[1,896,512]{1,2,0:T(8,128)(2,1)} %copy.14) | copy-start | bytes 2752516
Sparse Core Ops, SparseCore 0:
  53.7 64.7 reduce-scatter.4
  154.2 7.0 reduce-scatter.6
  163.6 15.8 reduce-scatter.8
  183.1 49.2 reduce-scatter.10
where the time goes:
time: 244 us
  waiting for transfers between devices  126 us (52%)
  blocking collectives  77.5 us (32%)
  between operations  13.9 us (6%)
  matrix products  9.92 us (4%)
  other arithmetic  8.57 us (4%)
  local copies, waits for them, and re-layouts  8.15 us (3%)
    reduce_scatter x1, waiting for transfers between devices, local(): lax.psum_scatter(dec_scale * jnp.dot(picked, flat_blocks, preferred_eleme...  64.8 us
    reduce_scatter x1, waiting for transfers between devices, local(): lax.psum_scatter(enc_grad, 'dp', scatter_dimension=0, tiled=True)  35.5 us
    all_gather x1, blocking collectives, local(): inputs = lax.all_gather(resid[0], 'feat', axis=1, tiled=True)  33.2 us
    all_gather x1, blocking collectives, local(): errors = lax.all_gather(local_errors, 'feat', axis=0, tiled=True)  31.3 us
    reduce_scatter x1, waiting for transfers between devices, local(): lax.psum_scatter(by_layer, 'dp', scatter_dimension=0, tiled=True)[:, 0, :]  18.1 us
    reduce_scatter x1, waiting for transfers between devices, local(): lax.psum_scatter(terms * alive[None, :, None].astype(jnp.float32), 'layer...  7.19 us
    unnamed x22, local copies, waits for them, and re-layouts  6.78 us
    all_gather x1, blocking collectives, local(): token_codes = lax.all_gather(codes, 'dp', axis=0, tiled=True)  5.62 us
  transfers between devices with their start and end apart: 4, of which 4 were waited for; matrix products, arithmetic and copies ran while one was open for 3% of the time, Pallas kernels for 0%

commit v1 on v0

--- a/solution.py
+++ b/solution.py
@@ -1,10 +1,16 @@
+import functools
+
 import jax
 import jax.numpy as jnp
 from jax import lax
+from jax.experimental import pallas as pl
+from jax.experimental.pallas import tpu as pltpu
 from jax.sharding import PartitionSpec as P
 
 step_weight = 256.0
 step_bias = 4.0
+bf16 = jnp.bfloat16
+f32 = jnp.float32
 
 
 def contract_rows(left, right):
@@ -19,7 +25,254 @@
     )
 
 
-def local(resid, target, enc_weight, enc_bias, dec_weight, dec_bias):
+def dot(left, right):
+    return jnp.dot(left, right, preferred_element_type=jnp.float32)
+
+
+def call(body, name, out_shape, *operands):
+    return pl.pallas_call(body, out_shape=out_shape, name=name)(*operands)
+
+
+def near(low):
+    return range(4) if low else range(1, 4)
+
+
+def swap_feat(value, mask):
+    count = lax.axis_size("feat")
+    return lax.ppermute(value, "feat", [(i, i ^ mask) for i in range(count)])
+
+
+def swap_dp(value):
+    return lax.ppermute(value, "dp", [(0, 1), (1, 0)])
+
+
+def aligned(i, size):
+    return pl.ds(pl.multiple_of(i * size, size), size)
+
+
+def encode_body(scale, near0, near1, near2, near3, weight, bias, codes, halves):
+    feat = lax.axis_index("feat")
+    dp = lax.axis_index("dp")
+    far, _, depth = near0.shape
+    own_first = far // 2 * ((feat // (2 * far) + 1 - dp) % 2)
+    total = None
+    for s, blocks in enumerate((near0, near1, near2, near3)):
+        for t in range(far):
+            source = feat ^ (s + 4 * t)
+            part = dot(blocks[t], weight[0, aligned(source, depth), :])
+            total = part if total is None else total + part
+        for u in range(far // 2):
+            halves[s, u] = blocks[own_first + u]
+    codes[...] = jnp.maximum(scale * total + bias[...], 0.0).astype(bf16)
+
+
+def decode_body(scale, layers, *refs):
+    own, partner = refs[:2]
+    from_own = refs[2 : 1 + layers]
+    from_partner = refs[1 + layers : 2 * layers]
+    weight = refs[2 * layers]
+    keep, send1, send2, send3, stacked, total = refs[2 * layers + 1 :]
+    layer = lax.axis_index("layer")
+    quarter = lax.axis_index("feat") % 4
+    rows = own.shape[0]
+    for half, parts in enumerate(((own, *from_own), (partner, *from_partner))):
+        result = None
+        for shift, codes in enumerate(parts):
+            stacked[shift, half * rows : (half + 1) * rows, :] = codes[...]
+            source = (layer + layers - shift) % layers
+            part = dot(codes[...], weight[0, source])
+            result = part if result is None else result + part
+        total[...] = scale * result
+        _, groups, block, _ = keep.shape
+        for g in range(groups):
+            keep[half, g] = total[aligned(4 * g + quarter, block), :]
+            for s, send in ((1, send1), (2, send2), (3, send3)):
+                send[half, g] = total[aligned(4 * g + (quarter ^ s), block), :].astype(bf16)
+
+
+def add_body(keep, one, two, three, out):
+    out[...] = (
+        (keep[...] + one[...].astype(f32)) + (two[...].astype(f32) + three[...].astype(f32))
+    ).astype(bf16)
+
+
+def error_body(first, second, targets, bias, errors):
+    far_own = lax.axis_index("feat") // 4
+    dp = lax.axis_index("dp")
+    _, groups, _, _ = first.shape
+    for half in range(2):
+        for g in range(groups):
+            far = (dp ^ half) * groups + g
+            recon = first[half, g].astype(f32) + second[half, g].astype(f32) + bias[...]
+            errors[half, g] = (recon - targets[far ^ far_own].astype(f32)).astype(bf16)
+
+
+def back_body(scale, rate, layers, *refs):
+    near_errors = refs[:4]
+    weight, bias = refs[4:6]
+    errors, new_bias = refs[6:8]
+    terms = refs[8:]
+    layer = lax.axis_index("layer")
+    quarter = lax.axis_index("feat") % 4
+    _, groups, block, _ = near_errors[0].shape
+    for half in range(2):
+        for g in range(groups):
+            for s, source in enumerate(near_errors):
+                errors[aligned((half * groups + g) * 4 + (quarter ^ s), block), :] = source[half, g]
+    value = errors[...]
+    for shift, term in enumerate(terms, 1):
+        source = (layer + layers - shift) % layers
+        term[...] = (scale * contract_width(value, weight[0, source])).astype(bf16)
+    new_bias[...] = bias[...] - rate * jnp.sum(value.astype(f32), axis=0, keepdims=True)
+
+
+def own_body(scale, layers, errors, weight, *refs):
+    total = scale * contract_width(errors[...], weight[0, lax.axis_index("layer")])
+    for received in refs[:-1]:
+        total = total + received[...].astype(f32)
+    refs[-1][...] = total.astype(bf16)
+
+
+def decoder_body(scale, layers, stacked, errors, weight, new_weight):
+    layer = lax.axis_index("layer")
+    shift = (layer + layers - pl.program_id(0)) % layers
+    columns = pl.program_id(1)
+    width = new_weight.shape[2]
+    codes = stacked[shift, :, aligned(columns, width)] if False else stacked[shift]
+    grad = contract_rows(codes, errors[...])
+    new_weight[0, 0] = (weight[0, 0].astype(f32) - scale * grad).astype(bf16)
+
+
+def encoder_body(
+    scale, near0, near1, near2, near3, others, codes, term, other_term, weight, bias, new_weight,
+    new_bias
+):
+    feat = lax.axis_index("feat")
+    dp = lax.axis_index("dp")
+    far, rows, depth = near0.shape
+    first = far // 2 * ((feat // (2 * far) + dp) % 2)
+    grads = []
+    sums = []
+    for half in range(2):
+        mine = slice(half * rows, (half + 1) * rows)
+        theirs = slice((1 - half) * rows, (2 - half) * rows)
+        summed = term[mine, :].astype(f32) + other_term[theirs, :].astype(f32)
+        alive = codes[0, mine, :].astype(f32) > 0.0
+        grad = jnp.where(alive, summed, 0.0).astype(bf16)
+        grads.append(grad)
+        sums.append(jnp.sum(grad.astype(f32), axis=0, keepdims=True))
+    new_bias[...] = bias[...] - step_bias * (sums[0] + sums[1])
+    for s, blocks in enumerate((near0, near1, near2, near3)):
+        for u in range(far // 2):
+            grad = contract_rows(blocks[first + u], grads[0]) + contract_rows(others[s, u], grads[1])
+            source = (feat ^ (s + 4 * u)) % (2 * far)
+            old = weight[0, aligned(dp * 2 * far + source, depth), :]
+            new_weight[0, aligned(source, depth), :] = (old.astype(f32) - scale * grad).astype(bf16)
+
+
+def shape(dims, dtype):
+    return jax.ShapeDtypeStruct(dims, dtype)
+
+
+def exchange(resid, target, enc_weight, enc_bias, dec_weight, dec_bias):
+    layers = lax.axis_size("layer")
+    count = lax.axis_size("feat")
+    _, rows, depth = resid.shape
+    _, width, feat_dev = enc_weight.shape
+    half_width = dec_weight.shape[3]
+    row_count = rows * lax.axis_size("dp")
+    far = count // 4
+    block = row_count // count
+    enc_scale = width ** (-0.5)
+    dec_scale = (feat_dev * count) ** (-0.5)
+    scale_rows = dec_scale / row_count
+
+    near0 = resid
+    targets = target
+    bit = 4
+    while bit < count:
+        near0 = jnp.concatenate([near0, swap_feat(near0, bit)])
+        bit *= 2
+    inputs = [near0] + [swap_feat(near0, s) for s in range(1, 4)]
+    codes, halves = call(
+        functools.partial(encode_body, enc_scale),
+        "encode",
+        (shape((rows, feat_dev), bf16), shape((4, far // 2, rows, depth), bf16)),
+        *inputs, enc_weight, enc_bias,
+    )
+    bit = 4
+    while bit < count:
+        targets = jnp.concatenate([targets, swap_feat(targets, bit)])
+        bit *= 2
+
+    def to_later(value, shift):
+        return lax.ppermute(value, "layer", [(i, i + shift) for i in range(layers - shift)])
+
+    partner = swap_dp(codes)
+    from_own = [to_later(codes, shift) for shift in range(1, layers)]
+    from_partner = [to_later(partner, shift) for shift in range(1, layers)]
+    groups = far // 2
+    piece = (2, groups, block, half_width)
+    keep, *sends, stacked = pl.pallas_call(
+        functools.partial(decode_body, dec_scale, layers),
+        out_shape=(
+            shape(piece, f32), shape(piece, bf16), shape(piece, bf16), shape(piece, bf16),
+            shape((layers, row_count, feat_dev), bf16),
+        ),
+        scratch_shapes=[pltpu.VMEM((rows, half_width), f32)],
+        name="decode",
+    )(codes, partner, *from_own, *from_partner, dec_weight)
+    others = swap_dp(halves)
+    received = [swap_feat(send, s) for s, send in enumerate(sends, 1)]
+    partial = call(add_body, "add", shape(piece, bf16), keep, *received)
+    bit = 4
+    while 2 * bit < count:
+        partial = (partial.astype(f32) + swap_feat(partial, bit).astype(f32)).astype(bf16)
+        bit *= 2
+    local_errors = call(
+        error_body, "errors", shape(piece, bf16), partial, swap_feat(partial, bit), targets, dec_bias
+    )
+    near_errors = [local_errors] + [swap_feat(local_errors, s) for s in range(1, 4)]
+    errors, new_dec_bias, *terms = call(
+        functools.partial(back_body, scale_rows, step_bias / row_count, layers),
+        "back",
+        (shape((row_count, half_width), bf16), shape((1, half_width), f32))
+        + (shape((row_count, feat_dev), bf16),) * (layers - 1),
+        *near_errors, dec_weight, dec_bias,
+    )
+    from_later = [
+        lax.ppermute(term, "layer", [(i + shift, i) for i in range(layers - shift)])
+        for shift, term in enumerate(terms, 1)
+    ]
+    term = call(
+        functools.partial(own_body, scale_rows, layers),
+        "own_term",
+        shape((row_count, feat_dev), bf16),
+        errors, dec_weight, *from_later,
+    )
+    other_term = swap_dp(term)
+    new_dec_weight = pl.pallas_call(
+        functools.partial(decoder_body, step_weight * scale_rows, layers),
+        out_shape=shape(dec_weight.shape, bf16),
+        grid=(layers, 1),
+        in_specs=[
+            pl.BlockSpec(stacked.shape, lambda i, j: (0, 0, 0)),
+            pl.BlockSpec(errors.shape, lambda i, j: (0, 0)),
+            pl.BlockSpec((1, 1, feat_dev, half_width), lambda i, j: (0, i, 0, 0)),
+        ],
+        out_specs=pl.BlockSpec((1, 1, feat_dev, half_width), lambda i, j: (0, i, 0, 0)),
+        name="decoder_step",
+    )(stacked, errors, dec_weight)
+    new_enc_weight, new_enc_bias = call(
+        functools.partial(encoder_body, step_weight * enc_scale),
+        "encoder_step",
+        (shape((1, width // 2, feat_dev), bf16), shape((1, feat_dev), f32)),
+        *inputs, others, stacked, term, other_term, enc_weight, enc_bias,
+    )
+    return new_enc_weight, new_enc_bias, new_dec_weight, new_dec_bias
+
+
+def general(resid, target, enc_weight, enc_bias, dec_weight, dec_bias):
     layer_count = lax.axis_size("layer")
     layer_index = lax.axis_index("layer")
     width = enc_weight.shape[1]
@@ -43,9 +296,8 @@
         row_count, layer_count * feat_dev
     )
     flat_blocks = blocks.reshape(layer_count * feat_dev, half_width)
-    picked = masked_codes
     summed = lax.psum_scatter(
-        dec_scale * jnp.dot(picked, flat_blocks, preferred_element_type=jnp.float32),
+        dec_scale * jnp.dot(masked_codes, flat_blocks, preferred_element_type=jnp.float32),
         "feat",
         scatter_dimension=0,
         tiled=True,
@@ -58,8 +310,7 @@
     )
     new_blocks = (blocks.astype(jnp.float32) - step_weight * dec_grad).astype(jnp.bfloat16)
     new_dec_bias = dec_bias[0] - step_bias * jnp.sum(errors.astype(jnp.float32), axis=0) / row_count
-    picked = errors
-    terms = scale_rows * contract_width(picked, flat_blocks).reshape(
+    terms = scale_rows * contract_width(errors, flat_blocks).reshape(
         row_count, layer_count, feat_dev
     )
     by_layer = lax.psum_scatter(
@@ -72,20 +323,27 @@
     dp_count = lax.axis_size("dp")
     dp_index = lax.axis_index("dp")
     share = width // dp_count
-    enc_part, bias_rows = (
-        lax.psum_scatter(enc_grad, "dp", scatter_dimension=0, tiled=True),
-        lax.psum_scatter(
-            jnp.broadcast_to(bias_grad[None, :], (dp_count, feat_dev)),
-            "dp",
-            scatter_dimension=0,
-            tiled=True,
-        ),
-    )
-    bias_total = bias_rows[0]
+    enc_part = lax.psum_scatter(enc_grad, "dp", scatter_dimension=0, tiled=True)
+    bias_total = lax.psum(bias_grad, "dp")
     old_part = lax.dynamic_slice_in_dim(enc_weight[0], dp_index * share, share, 0)
     new_enc = (old_part.astype(jnp.float32) - step_weight * enc_part).astype(jnp.bfloat16)
     new_enc_bias = enc_bias[0] - step_bias * bias_total
     return (new_enc[None], new_enc_bias[None], new_blocks[None], new_dec_bias[None])
+
+
+def local(*operands):
+    resid, target, enc_weight, _, dec_weight, _ = operands
+    count = lax.axis_size("feat")
+    fits = (
+        lax.axis_size("dp") == 2
+        and count >= 8
+        and count & (count - 1) == 0
+        and resid.shape[2] % 32 == 0
+        and target.shape[1] % 32 == 0
+        and enc_weight.shape[2] % 128 == 0
+        and dec_weight.shape[3] % 128 == 0
+    )
+    return exchange(*operands) if fits else general(*operands)
 
 
 def solution(mesh):

time: 244 us -> 94.5 us (0.39)
  waiting for transfers between devices: 126 us -> 35.1 us
  blocking collectives: 77.5 us -> 0 us
  starting transfers between devices: 0.16 us -> 28.2 us
  Pallas kernels: 0 us -> 22.8 us
  between operations: 13.9 us -> 0.75 us
  matrix products: 9.92 us -> 0 us
  other arithmetic: 8.57 us -> 0.69 us
    reduce_scatter x4 -> x0, waiting for transfers between devices: 126 us -> none  [the longest x1 64.8 us: local(): lax.psum_scatter(dec_scale * jnp.dot(picked, flat_blocks, preferred_eleme...]
    all_gather x4 -> x0, blocking collectives: 72.3 us -> none  [the longest x1 33.2 us: local(): inputs = lax.all_gather(resid[0], 'feat', axis=1, tiled=True)]
    ppermute x0 -> x18, waiting for transfers between devices: none -> 35.1 us  [the longest x12 20.7 us: swap_feat(): return lax.ppermute(value, 'feat', [(i, i ^ mask) for i in range(count)])]
    ppermute x0 -> x18, starting transfers between devices: none -> 28.2 us  [the longest x12 20.7 us: swap_feat(): return lax.ppermute(value, 'feat', [(i, i ^ mask) for i in range(count)])]
    pallas_call x0 -> x8, Pallas kernels: none -> 22.8 us  [the longest x6 16 us: call(): return pl.pallas_call(body, out_shape=out_shape, name=name)(*operands)]
    dot_general x5 -> x0, matrix products: 9.92 us -> none  [the longest x1 3.25 us: contract_width(): lax.dot_general(left, right, (((1,), (1,)), ((), ())), preferred_element_...]
    unnamed x1 -> x0, blocking collectives: 5.12 us -> none
    broadcast_in_dim x1 -> x0, other arithmetic: 2.64 us -> none  [local(): new_enc[None]]
  transfers between devices with their start and end apart: 4 -> 18, of which waited for: 4 -> 13; matrix products, arithmetic and copies ran while one was open for 3% -> 1% of each run, Pallas kernels for 0% -> 5%
where the time goes in v1:
time: 94.5 us; the launch traced here: 94 us
  waiting for transfers between devices  35.1 us (37%)
  starting transfers between devices  28.2 us (30%)
  Pallas kernels  22.8 us (24%)
  local copies, waits for them, and re-layouts  6.42 us (7%)
    ppermute x12, starting transfers between devices, swap_feat(): return lax.ppermute(value, 'feat', [(i, i ^ mask) for i in range(count)])  20.7 us
    ppermute x12, waiting for transfers between devices, swap_feat(): return lax.ppermute(value, 'feat', [(i, i ^ mask) for i in range(count)])  20.7 us
    pallas_call x6, Pallas kernels, call(): return pl.pallas_call(body, out_shape=out_shape, name=name)(*operands)  16 us
    ppermute x3, waiting for transfers between devices, swap_dp(): return lax.ppermute(value, 'dp', [(0, 1), (1, 0)])  11.2 us
    unnamed x39, local copies, waits for them, and re-layouts  6.42 us
    ppermute x3, starting transfers between devices, swap_dp(): return lax.ppermute(value, 'dp', [(0, 1), (1, 0)])  3.54 us
    pallas_call x1, Pallas kernels, exchange(): pl.pallas_call(functools.partial(decode_body, dec_scale, layers), out_sha...  3.48 us
    pallas_call x1, Pallas kernels, exchange(): pl.pallas_call(functools.partial(decoder_body, step_weight * scale_rows,...  3.36 us
  transfers between devices with their start and end apart: 18, of which 13 were waited for; matrix products, arithmetic and copies ran while one was open for 1% of the time, Pallas kernels for 5%

profile of v1, /device:TPU:0, one launch (start us, length us, event | category | flops | bytes accessed | tf_op | source)
XLA Modules:
  0.0 94.0 jit_solution(5395569197795768723)
XLA Ops:
  1.6 4.1 %collective-permute-start = (bf16[1,128,224]{2,1,0:T(8,128)(2,1)S(1)}, bf16[1,128,224]{2,1,0:T(8,128)(2,1)S(1)}, u32[]{:S(2)}, u32[]{:S(2)}) collective-permute-start(bf16[1,128,224]{2,1,0:T(8,128)(2,1)S(1)} %copy.11), channel_id=1, source_target_pairs={{0,8},{2,10},{4,12},{6,14},{8,0},{10,2},{12,4},{14,6},{1,9},{3,11}... | collective-permute-start | bytes 172040 | tf_op jit(solution)/shard_map/ppermute | solution.py:42
  5.7 3.6 %collective-permute-done = bf16[1,128,224]{2,1,0:T(8,128)(2,1)S(1)} collective-permute-done((bf16[1,128,224]{2,1,0:T(8,128)(2,1)S(1)}, bf16[1,128,224]{2,1,0:T(8,128)(2,1)S(1)}, u32[]{:S(2)}, u32[]{:S(2)}) %collective-permute-start) | collective-permute-done | bytes 57376 | tf_op jit(solution)/shard_map/ppermute | solution.py:42
  9.4 1.6 %collective-permute-start.3 = (bf16[2,128,224]{2,1,0:T(8,128)(2,1)S(1)}, bf16[2,128,224]{2,1,0:T(8,128)(2,1)S(1)}, u32[]{:S(2)}, u32[]{:S(2)}) collective-permute-start(bf16[2,128,224]{2,1,0:T(8,128)(2,1)S(1)} %pad_maximum_fusion.near0), channel_id=1, source_target_pairs={{0,6},{2,4},{4,2},{6,0},{8,14},{10,12},{12,10},{14,8},{1,7},{3,5},... | collective-permute-start | bytes 344072 | tf_op jit(solution)/shard_map/ppermute | solution.py:42
  10.9 1.7 %collective-permute-start.2 = (bf16[2,128,224]{2,1,0:T(8,128)(2,1)S(1)}, bf16[2,128,224]{2,1,0:T(8,128)(2,1)S(1)}, u32[]{:S(2)}, u32[]{:S(2)}) collective-permute-start(bf16[2,128,224]{2,1,0:T(8,128)(2,1)S(1)} %pad_maximum_fusion.near0), channel_id=1, source_target_pairs={{0,4},{2,6},{4,0},{6,2},{8,12},{10,14},{12,8},{14,10},{1,5},{3,7},... | collective-permute-start | bytes 344072 | tf_op jit(solution)/shard_map/ppermute | solution.py:42
  12.9 2.7 %collective-permute-done.3.near3 = bf16[2,128,224]{2,1,0:T(8,128)(2,1)S(1)} collective-permute-done((bf16[2,128,224]{2,1,0:T(8,128)(2,1)S(1)}, bf16[2,128,224]{2,1,0:T(8,128)(2,1)S(1)}, u32[]{:S(2)}, u32[]{:S(2)}) %collective-permute-start.3) | collective-permute-done | bytes 114720 | tf_op jit(solution)/shard_map/ppermute | solution.py:42
  15.6 1.4 %collective-permute-done.2.near2 = bf16[2,128,224]{2,1,0:T(8,128)(2,1)S(1)} collective-permute-done((bf16[2,128,224]{2,1,0:T(8,128)(2,1)S(1)}, bf16[2,128,224]{2,1,0:T(8,128)(2,1)S(1)}, u32[]{:S(2)}, u32[]{:S(2)}) %collective-permute-start.2) | collective-permute-done | bytes 114720 | tf_op jit(solution)/shard_map/ppermute | solution.py:42
  18.3 2.9 %encode.1 = (bf16[128,512]{1,0:T(8,128)(2,1)}, bf16[4,1,128,224]{3,2,1,0:T(8,128)(2,1)}) custom-call(bf16[2,128,224]{2,1,0:T(8,128)(2,1)} %copy-done, bf16[2,128,224]{2,1,0:T(8,128)(2,1)} %copy-done.3, bf16[2,128,224]{2,1,0:T(8,128)(2,1)} %copy-done.2, bf16[2,128,224]{2,1,0:T(8,128)(2,1)} %copy-done.1, bf16[1,1792,512]{2,1,0:T(8,128)(2,1)} %weight.6, ...), custom_call_target="tpu_custom_call" | custom-call | tf_op jit(solution)/shard_map/encode/pallas_call | solution.py:33
  21.3 1.5 %collective-permute-start.5 = (bf16[128,512]{1,0:T(8,128)(2,1)}, bf16[128,512]{1,0:T(8,128)(2,1)S(1)}, u32[]{:S(2)}, u32[]{:S(2)}) collective-permute-start(bf16[128,512]{1,0:T(8,128)(2,1)} %get-tuple-element.17.refs_0_), channel_id=1, source_target_pairs={{0,1},{1,0},{2,3},{3,2},{4,5},{5,4},{6,7},{7,6},{8,9},{9,8},{10,11... | collective-permute-start | bytes 393224 | tf_op jit(solution)/shard_map/ppermute | solution.py:46
  22.8 1.3 %collective-permute-start.6 = (bf16[128,512]{1,0:T(8,128)(2,1)}, bf16[128,512]{1,0:T(8,128)(2,1)S(1)}, u32[]{:S(2)}, u32[]{:S(2)}) collective-permute-start(bf16[128,512]{1,0:T(8,128)(2,1)} %get-tuple-element.17.refs_0_), channel_id=1, source_target_pairs={{0,16},{1,17},{2,18},{3,19},{4,20},{5,21},{6,22},{7,23},{8,24},{9,... | collective-permute-start | bytes 393224 | tf_op jit(solution)/shard_map/ppermute | solution.py:209
  24.1 2.4 %collective-permute-done.5.refs_1_ = bf16[128,512]{1,0:T(8,128)(2,1)S(1)} collective-permute-done((bf16[128,512]{1,0:T(8,128)(2,1)}, bf16[128,512]{1,0:T(8,128)(2,1)S(1)}, u32[]{:S(2)}, u32[]{:S(2)}) %collective-permute-start.5) | collective-permute-done | bytes 131104 | tf_op jit(solution)/shard_map/ppermute | solution.py:46
  26.4 1.3 %collective-permute-start.7 = (bf16[128,512]{1,0:T(8,128)(2,1)S(1)}, bf16[128,512]{1,0:T(8,128)(2,1)S(1)}, u32[]{:S(2)}, u32[]{:S(2)}) collective-permute-start(bf16[128,512]{1,0:T(8,128)(2,1)S(1)} %collective-permute-done.5.refs_1_), channel_id=1, source_target_pairs={{0,16},{1,17},{2,18},{3,19},{4,20},{5,21},{6,22},{7,23},{8,24},{9,... | collective-permute-start | bytes 393224 | tf_op jit(solution)/shard_map/ppermute | solution.py:209
  27.8 0.9 %collective-permute-done.7.refs_3_ = bf16[128,512]{1,0:T(8,128)(2,1)S(1)} collective-permute-done((bf16[128,512]{1,0:T(8,128)(2,1)S(1)}, bf16[128,512]{1,0:T(8,128)(2,1)S(1)}, u32[]{:S(2)}, u32[]{:S(2)}) %collective-permute-start.7) | collective-permute-done | bytes 131104 | tf_op jit(solution)/shard_map/ppermute | solution.py:209
  29.3 3.5 %decode.1 = (f32[2,1,32,896]{3,2,1,0:T(8,128)}, bf16[2,1,32,896]{3,2,1,0:T(8,128)(2,1)}, bf16[2,1,32,896]{3,2,1,0:T(8,128)(2,1)}, bf16[2,1,32,896]{3,2,1,0:T(8,128)(2,1)}, bf16[2,256,512]{2,1,0:T(8,128)(2,1)}) custom-call(bf16[128,512]{1,0:T(8,128)(2,1)} %get-tuple-element.17.refs_0_, bf16[128,512]{1,0:T(8,128)(2,1)} %copy-done.7, ...), custom_call_target="tpu_custom_call" | custom-call | tf_op jit(solution)/shard_map/decode/pallas_call | solution.py:216
  33.6 1.7 %collective-permute-start.9 = (bf16[2,1,32,896]{3,2,1,0:T(8,128)(2,1)}, bf16[2,1,32,896]{3,2,1,0:T(8,128)(2,1)S(1)}, u32[]{:S(2)}, u32[]{:S(2)}) collective-permute-start(bf16[2,1,32,896]{3,2,1,0:T(8,128)(2,1)} %get-tuple-element.21), channel_id=1, source_target_pairs={{0,4},{2,6},{4,0},{6,2},{8,12},{10,14},{12,8},{14,10},{1,5},{3,7},... | collective-permute-start | bytes 344072 | tf_op jit(solution)/shard_map/ppermute | solution.py:42
  35.3 1.0 %collective-permute-start.10 = (bf16[2,1,32,896]{3,2,1,0:T(8,128)(2,1)}, bf16[2,1,32,896]{3,2,1,0:T(8,128)(2,1)S(1)}, u32[]{:S(2)}, u32[]{:S(2)}) collective-permute-start(bf16[2,1,32,896]{3,2,1,0:T(8,128)(2,1)} %get-tuple-element.22), channel_id=1, source_target_pairs={{0,6},{2,4},{4,2},{6,0},{8,14},{10,12},{12,10},{14,8},{1,7},{3,5},... | collective-permute-start | bytes 344072 | tf_op jit(solution)/shard_map/ppermute | solution.py:42
  36.3 3.2 %collective-permute-start.12 = (bf16[1,32,896]{2,1,0:T(8,128)(2,1)S(1)}, bf16[1,32,896]{2,1,0:T(8,128)(2,1)S(1)}, u32[]{:S(2)}, u32[]{:S(2)}) collective-permute-start(bf16[1,32,896]{2,1,0:T(8,128)(2,1)S(1)} %copy-done.17), channel_id=1, source_target_pairs={{0,8},{2,10},{4,12},{6,14},{8,0},{10,2},{12,4},{14,6},{1,9},{3,11}... | collective-permute-start | bytes 172040 | tf_op jit(solution)/shard_map/ppermute | solution.py:42
  39.5 3.8 %collective-permute-done.10.three = bf16[2,1,32,896]{3,2,1,0:T(8,128)(2,1)S(1)} collective-permute-done((bf16[2,1,32,896]{3,2,1,0:T(8,128)(2,1)}, bf16[2,1,32,896]{3,2,1,0:T(8,128)(2,1)S(1)}, u32[]{:S(2)}, u32[]{:S(2)}) %collective-permute-start.10) | collective-permute-done | bytes 114720 | tf_op jit(solution)/shard_map/ppermute | solution.py:42
  44.0 1.8 %add.1.first = bf16[2,1,32,896]{3,2,1,0:T(8,128)(2,1)} custom-call(f32[2,1,32,896]{3,2,1,0:T(8,128)} %get-tuple-element.19.keep, bf16[2,1,32,896]{3,2,1,0:T(8,128)(2,1)} %copy-done.11, bf16[2,1,32,896]{3,2,1,0:T(8,128)(2,1)} %copy-done.12, bf16[2,1,32,896]{3,2,1,0:T(8,128)(2,1)} %copy-done.14), custom_call_target="tpu_custom_call" | custom-call | tf_op jit(solution)/shard_map/add/pallas_call | solution.py:33
  45.8 2.8 %collective-permute-start.11 = (bf16[2,1,32,896]{3,2,1,0:T(8,128)(2,1)}, bf16[2,1,32,896]{3,2,1,0:T(8,128)(2,1)S(1)}, u32[]{:S(2)}, u32[]{:S(2)}) collective-permute-start(bf16[2,1,32,896]{3,2,1,0:T(8,128)(2,1)} %add.1.first), channel_id=1, source_target_pairs={{0,8},{2,10},{4,12},{6,14},{8,0},{10,2},{12,4},{14,6},{1,9},{3,11}... | collective-permute-start | bytes 344072 | tf_op jit(solution)/shard_map/ppermute | solution.py:42
  49.3 4.9 %collective-permute-done.11.second = bf16[2,1,32,896]{3,2,1,0:T(8,128)(2,1)S(1)} collective-permute-done((bf16[2,1,32,896]{3,2,1,0:T(8,128)(2,1)}, bf16[2,1,32,896]{3,2,1,0:T(8,128)(2,1)S(1)}, u32[]{:S(2)}, u32[]{:S(2)}) %collective-permute-start.11) | collective-permute-done | bytes 114720 | tf_op jit(solution)/shard_map/ppermute | solution.py:42
  54.8 1.7 %errors.1.refs_0_ = bf16[2,1,32,896]{3,2,1,0:T(8,128)(2,1)} custom-call(bf16[2,1,32,896]{3,2,1,0:T(8,128)(2,1)} %add.1.first, bf16[2,1,32,896]{3,2,1,0:T(8,128)(2,1)} %copy-done.10, bf16[2,32,896]{2,1,0:T(8,128)(2,1)} %pad_maximum_fusion.1.targets, f32[1,896]{1,0:T(1,128)} %refs_5_.1), custom_call_target="tpu_custom_call" | custom-call | tf_op jit(solution)/shard_map/errors/pallas_call | solution.py:33
  56.9 1.8 %collective-permute-start.14 = (bf16[2,1,32,896]{3,2,1,0:T(8,128)(2,1)}, bf16[2,1,32,896]{3,2,1,0:T(8,128)(2,1)S(1)}, u32[]{:S(2)}, u32[]{:S(2)}) collective-permute-start(bf16[2,1,32,896]{3,2,1,0:T(8,128)(2,1)} %errors.1.refs_0_), channel_id=1, source_target_pairs={{0,4},{2,6},{4,0},{6,2},{8,12},{10,14},{12,8},{14,10},{1,5},{3,7},... | collective-permute-start | bytes 344072 | tf_op jit(solution)/shard_map/ppermute | solution.py:42
  58.7 1.3 %collective-permute-start.13 = (bf16[2,1,32,896]{3,2,1,0:T(8,128)(2,1)}, bf16[2,1,32,896]{3,2,1,0:T(8,128)(2,1)S(1)}, u32[]{:S(2)}, u32[]{:S(2)}) collective-permute-start(bf16[2,1,32,896]{3,2,1,0:T(8,128)(2,1)} %errors.1.refs_0_), channel_id=1, source_target_pairs={{0,2},{2,0},{4,6},{6,4},{8,10},{10,8},{12,14},{14,12},{1,3},{3,1},... | collective-permute-start | bytes 344072 | tf_op jit(solution)/shard_map/ppermute | solution.py:42
  60.0 2.4 %collective-permute-done.15.refs_3_ = bf16[2,1,32,896]{3,2,1,0:T(8,128)(2,1)S(1)} collective-permute-done((bf16[2,1,32,896]{3,2,1,0:T(8,128)(2,1)}, bf16[2,1,32,896]{3,2,1,0:T(8,128)(2,1)S(1)}, u32[]{:S(2)}, u32[]{:S(2)}) %collective-permute-start.15) | collective-permute-done | bytes 114720 | tf_op jit(solution)/shard_map/ppermute | solution.py:42
  64.4 2.9 %back.1 = (bf16[256,896]{1,0:T(8,128)(2,1)}, f32[1,896]{1,0:T(1,128)}, bf16[256,512]{1,0:T(8,128)(2,1)}) custom-call(bf16[2,1,32,896]{3,2,1,0:T(8,128)(2,1)} %errors.1.refs_0_, bf16[2,1,32,896]{3,2,1,0:T(8,128)(2,1)} %copy-done.16, bf16[2,1,32,896]{3,2,1,0:T(8,128)(2,1)} %copy-done.15, bf16[2,1,32,896]{3,2,1,0:T(8,128)(2,1)} %copy-done.13, ...), custom_call_target="tpu_custom_call" | custom-call | tf_op jit(solution)/shard_map/back/pallas_call | solution.py:33
  67.3 1.4 %collective-permute-start.16 = (bf16[256,512]{1,0:T(8,128)(2,1)}, bf16[256,512]{1,0:T(8,128)(2,1)S(1)}, u32[]{:S(2)}, u32[]{:S(2)}) collective-permute-start(bf16[256,512]{1,0:T(8,128)(2,1)} %get-tuple-element.24), channel_id=1, source_target_pairs={{16,0},{17,1},{18,2},{19,3},{20,4},{21,5},{22,6},{23,7},{24,8},{25... | collective-permute-start | bytes 786440 | tf_op jit(solution)/shard_map/ppermute | solution.py:244
  68.8 2.3 %collective-permute-done.16.refs_0_ = bf16[256,512]{1,0:T(8,128)(2,1)S(1)} collective-permute-done((bf16[256,512]{1,0:T(8,128)(2,1)}, bf16[256,512]{1,0:T(8,128)(2,1)S(1)}, u32[]{:S(2)}, u32[]{:S(2)}) %collective-permute-start.16) | collective-permute-done | bytes 262176 | tf_op jit(solution)/shard_map/ppermute | solution.py:244
  71.8 2.8 %own_term.1.term = bf16[256,512]{1,0:T(8,128)(2,1)} custom-call(bf16[256,896]{1,0:T(8,128)(2,1)} %get-tuple-element.23.errors, bf16[1,2,512,896]{3,2,1,0:T(8,128)(2,1)} %weight.7, bf16[256,512]{1,0:T(8,128)(2,1)} %copy-done.6), custom_call_target="tpu_custom_call" | custom-call | tf_op jit(solution)/shard_map/own_term/pallas_call | solution.py:33
  74.6 1.5 %collective-permute-start.17 = (bf16[256,512]{1,0:T(8,128)(2,1)}, bf16[256,512]{1,0:T(8,128)(2,1)S(1)}, u32[]{:S(2)}, u32[]{:S(2)}) collective-permute-start(bf16[256,512]{1,0:T(8,128)(2,1)} %own_term.1.term), channel_id=1, source_target_pairs={{0,1},{1,0},{2,3},{3,2},{4,5},{5,4},{6,7},{7,6},{8,9},{9,8},{10,11... | collective-permute-start | bytes 786440 | tf_op jit(solution)/shard_map/ppermute | solution.py:46
  76.6 3.4 %decoder_step.1 = bf16[1,2,512,896]{3,2,1,0:T(8,128)(2,1)} custom-call(bf16[2,256,512]{2,1,0:T(8,128)(2,1)} %get-tuple-element.18.codes.stacked, bf16[256,896]{1,0:T(8,128)(2,1)} %get-tuple-element.23.errors, bf16[1,2,512,896]{3,2,1,0:T(8,128)(2,1)} %weight.7), custom_call_target="tpu_custom_call" | custom-call | tf_op jit(solution)/shard_map/decoder_step/pallas_call | solution.py:254
  80.0 8.8 %collective-permute-done.4.others = bf16[4,1,128,224]{3,2,1,0:T(8,128)(2,1)S(1)} collective-permute-done((bf16[4,1,128,224]{3,2,1,0:T(8,128)(2,1)S(1)}, bf16[4,1,128,224]{3,2,1,0:T(8,128)(2,1)S(1)}, u32[]{:S(2)}, u32[]{:S(2)}) %collective-permute-start.4) | collective-permute-done | bytes 229408 | tf_op jit(solution)/shard_map/ppermute | solution.py:46
  90.2 3.8 %encoder_step.1 = (bf16[1,896,512]{2,1,0:T(8,128)(2,1)}, f32[1,512]{1,0:T(1,128)}) custom-call(bf16[2,128,224]{2,1,0:T(8,128)(2,1)} %copy-done, bf16[2,128,224]{2,1,0:T(8,128)(2,1)} %copy-done.3, bf16[2,128,224]{2,1,0:T(8,128)(2,1)} %copy-done.2, bf16[2,128,224]{2,1,0:T(8,128)(2,1)} %copy-done.1, bf16[4,1,128,224]{3,2,1,0:T(8,128)(2,1)} %copy-done.5, ...), custom_call_target="tpu_custom_call" | custom-call | tf_op jit(solution)/shard_map/encoder_step/pallas_call | solution.py:33
  (53 shorter events, 11.1 us)
Async XLA Ops:
  1.6 7.8 %collective-permute-start = (bf16[1,128,224]{2,1,0:T(8,128)(2,1)S(1)}, bf16[1,128,224]{2,1,0:T(8,128)(2,1)S(1)}, u32[]{:S(2)}, u32[]{:S(2)}) collective-permute-start(bf16[1,128,224]{2,1,0:T(8,128)(2,1)S(1)} %copy.11), channel_id=1, source_target_pairs={{0,8},{2,10},{4,12},{6,14},{8,0},{10,2},{12,4},{14,6},{1,9},{3,11}... | collective-permute-start | bytes 172040 | tf_op jit(solution)/shard_map/ppermute | solution.py:42
  9.4 8.2 %copy-start = (bf16[2,128,224]{2,1,0:T(8,128)(2,1)}, bf16[2,128,224]{2,1,0:T(8,128)(2,1)S(1)}, u32[]{:S(2)}) copy-start(bf16[2,128,224]{2,1,0:T(8,128)(2,1)S(1)} %pad_maximum_fusion.near0) | copy-start | bytes 344068
  9.4 26.9 %copy-start.17 = (bf16[1,32,896]{2,1,0:T(8,128)(2,1)S(1)}, bf16[1,32,896]{2,1,0:T(8,128)(2,1)}, u32[]{:S(2)}) copy-start(bf16[1,32,896]{2,1,0:T(8,128)(2,1)} %param.7) | copy-start | bytes 172036
  9.4 6.2 %collective-permute-start.3 = (bf16[2,128,224]{2,1,0:T(8,128)(2,1)S(1)}, bf16[2,128,224]{2,1,0:T(8,128)(2,1)S(1)}, u32[]{:S(2)}, u32[]{:S(2)}) collective-permute-start(bf16[2,128,224]{2,1,0:T(8,128)(2,1)S(1)} %pad_maximum_fusion.near0), channel_id=1, source_target_pairs={{0,6},{2,4},{4,2},{6,0},{8,14},{10,12},{12,10},{14,8},{1,7},{3,5},... | collective-permute-start | bytes 344072 | tf_op jit(solution)/shard_map/ppermute | solution.py:42
  10.9 6.1 %collective-permute-start.2 = (bf16[2,128,224]{2,1,0:T(8,128)(2,1)S(1)}, bf16[2,128,224]{2,1,0:T(8,128)(2,1)S(1)}, u32[]{:S(2)}, u32[]{:S(2)}) collective-permute-start(bf16[2,128,224]{2,1,0:T(8,128)(2,1)S(1)} %pad_maximum_fusion.near0), channel_id=1, source_target_pairs={{0,4},{2,6},{4,0},{6,2},{8,12},{10,14},{12,8},{14,10},{1,5},{3,7},... | collective-permute-start | bytes 344072 | tf_op jit(solution)/shard_map/ppermute | solution.py:42
  12.6 5.0 %collective-permute-start.1 = (bf16[2,128,224]{2,1,0:T(8,128)(2,1)S(1)}, bf16[2,128,224]{2,1,0:T(8,128)(2,1)S(1)}, u32[]{:S(2)}, u32[]{:S(2)}) collective-permute-start(bf16[2,128,224]{2,1,0:T(8,128)(2,1)S(1)} %pad_maximum_fusion.near0), channel_id=1, source_target_pairs={{0,2},{2,0},{4,6},{6,4},{8,10},{10,8},{12,14},{14,12},{1,3},{3,1},... | collective-permute-start | bytes 344072 | tf_op jit(solution)/shard_map/ppermute | solution.py:42
  15.6 2.0 %copy-start.1 = (bf16[2,128,224]{2,1,0:T(8,128)(2,1)}, bf16[2,128,224]{2,1,0:T(8,128)(2,1)S(1)}, u32[]{:S(2)}) copy-start(bf16[2,128,224]{2,1,0:T(8,128)(2,1)S(1)} %collective-permute-done.3.near3) | copy-start | bytes 344068
  17.7 0.7 copy-start.3
  21.3 5.2 %collective-permute-start.5 = (bf16[128,512]{1,0:T(8,128)(2,1)}, bf16[128,512]{1,0:T(8,128)(2,1)S(1)}, u32[]{:S(2)}, u32[]{:S(2)}) collective-permute-start(bf16[128,512]{1,0:T(8,128)(2,1)} %get-tuple-element.17.refs_0_), channel_id=1, source_target_pairs={{0,1},{1,0},{2,3},{3,2},{4,5},{5,4},{6,7},{7,6},{8,9},{9,8},{10,11... | collective-permute-start | bytes 393224 | tf_op jit(solution)/shard_map/ppermute | solution.py:46
  22.8 5.0 %collective-permute-start.6 = (bf16[128,512]{1,0:T(8,128)(2,1)}, bf16[128,512]{1,0:T(8,128)(2,1)S(1)}, u32[]{:S(2)}, u32[]{:S(2)}) collective-permute-start(bf16[128,512]{1,0:T(8,128)(2,1)} %get-tuple-element.17.refs_0_), channel_id=1, source_target_pairs={{0,16},{1,17},{2,18},{3,19},{4,20},{5,21},{6,22},{7,23},{8,24},{9,... | collective-permute-start | bytes 393224 | tf_op jit(solution)/shard_map/ppermute | solution.py:209
  26.4 2.3 %copy-start.7 = (bf16[128,512]{1,0:T(8,128)(2,1)}, bf16[128,512]{1,0:T(8,128)(2,1)S(1)}, u32[]{:S(2)}) copy-start(bf16[128,512]{1,0:T(8,128)(2,1)S(1)} %collective-permute-done.5.refs_1_) | copy-start | bytes 393220
  26.4 2.3 %collective-permute-start.7 = (bf16[128,512]{1,0:T(8,128)(2,1)S(1)}, bf16[128,512]{1,0:T(8,128)(2,1)S(1)}, u32[]{:S(2)}, u32[]{:S(2)}) collective-permute-start(bf16[128,512]{1,0:T(8,128)(2,1)S(1)} %collective-permute-done.5.refs_1_), channel_id=1, source_target_pairs={{0,16},{1,17},{2,18},{3,19},{4,20},{5,21},{6,22},{7,23},{8,24},{9,... | collective-permute-start | bytes 393224 | tf_op jit(solution)/shard_map/ppermute | solution.py:209
  27.7 1.0 %copy-start.8 = (bf16[128,512]{1,0:T(8,128)(2,1)}, bf16[128,512]{1,0:T(8,128)(2,1)S(1)}, u32[]{:S(2)}) copy-start(bf16[128,512]{1,0:T(8,128)(2,1)S(1)} %collective-permute-done.6.refs_2_) | copy-start | bytes 393220
  32.8 6.7 %collective-permute-start.8 = (bf16[2,1,32,896]{3,2,1,0:T(8,128)(2,1)}, bf16[2,1,32,896]{3,2,1,0:T(8,128)(2,1)S(1)}, u32[]{:S(2)}, u32[]{:S(2)}) collective-permute-start(bf16[2,1,32,896]{3,2,1,0:T(8,128)(2,1)} %get-tuple-element.20), channel_id=1, source_target_pairs={{0,2},{2,0},{4,6},{6,4},{8,10},{10,8},{12,14},{14,12},{1,3},{3,1},... | collective-permute-start | bytes 344072 | tf_op jit(solution)/shard_map/ppermute | solution.py:42
  33.6 5.9 %collective-permute-start.9 = (bf16[2,1,32,896]{3,2,1,0:T(8,128)(2,1)}, bf16[2,1,32,896]{3,2,1,0:T(8,128)(2,1)S(1)}, u32[]{:S(2)}, u32[]{:S(2)}) collective-permute-start(bf16[2,1,32,896]{3,2,1,0:T(8,128)(2,1)} %get-tuple-element.21), channel_id=1, source_target_pairs={{0,4},{2,6},{4,0},{6,2},{8,12},{10,14},{12,8},{14,10},{1,5},{3,7},... | collective-permute-start | bytes 344072 | tf_op jit(solution)/shard_map/ppermute | solution.py:42
  35.3 8.0 %collective-permute-start.10 = (bf16[2,1,32,896]{3,2,1,0:T(8,128)(2,1)}, bf16[2,1,32,896]{3,2,1,0:T(8,128)(2,1)S(1)}, u32[]{:S(2)}, u32[]{:S(2)}) collective-permute-start(bf16[2,1,32,896]{3,2,1,0:T(8,128)(2,1)} %get-tuple-element.22), channel_id=1, source_target_pairs={{0,6},{2,4},{4,2},{6,0},{8,14},{10,12},{12,10},{14,8},{1,7},{3,5},... | collective-permute-start | bytes 344072 | tf_op jit(solution)/shard_map/ppermute | solution.py:42
  36.3 12.3 %collective-permute-start.12 = (bf16[1,32,896]{2,1,0:T(8,128)(2,1)S(1)}, bf16[1,32,896]{2,1,0:T(8,128)(2,1)S(1)}, u32[]{:S(2)}, u32[]{:S(2)}) collective-permute-start(bf16[1,32,896]{2,1,0:T(8,128)(2,1)S(1)} %copy-done.17), channel_id=1, source_target_pairs={{0,8},{2,10},{4,12},{6,14},{8,0},{10,2},{12,4},{14,6},{1,9},{3,11}... | collective-permute-start | bytes 172040 | tf_op jit(solution)/shard_map/ppermute | solution.py:42
  39.5 3.8 %copy-start.11 = (bf16[2,1,32,896]{3,2,1,0:T(8,128)(2,1)}, bf16[2,1,32,896]{3,2,1,0:T(8,128)(2,1)S(1)}, u32[]{:S(2)}) copy-start(bf16[2,1,32,896]{3,2,1,0:T(8,128)(2,1)S(1)} %collective-permute-done.8.one) | copy-start | bytes 344068
  39.5 3.8 %copy-start.12 = (bf16[2,1,32,896]{3,2,1,0:T(8,128)(2,1)}, bf16[2,1,32,896]{3,2,1,0:T(8,128)(2,1)S(1)}, u32[]{:S(2)}) copy-start(bf16[2,1,32,896]{3,2,1,0:T(8,128)(2,1)S(1)} %collective-permute-done.9.two) | copy-start | bytes 344068
  45.8 8.4 %collective-permute-start.11 = (bf16[2,1,32,896]{3,2,1,0:T(8,128)(2,1)}, bf16[2,1,32,896]{3,2,1,0:T(8,128)(2,1)S(1)}, u32[]{:S(2)}, u32[]{:S(2)}) collective-permute-start(bf16[2,1,32,896]{3,2,1,0:T(8,128)(2,1)} %add.1.first), channel_id=1, source_target_pairs={{0,8},{2,10},{4,12},{6,14},{8,0},{10,2},{12,4},{14,6},{1,9},{3,11}... | collective-permute-start | bytes 344072 | tf_op jit(solution)/shard_map/ppermute | solution.py:42
  56.5 5.9 %collective-permute-start.15 = (bf16[2,1,32,896]{3,2,1,0:T(8,128)(2,1)}, bf16[2,1,32,896]{3,2,1,0:T(8,128)(2,1)S(1)}, u32[]{:S(2)}, u32[]{:S(2)}) collective-permute-start(bf16[2,1,32,896]{3,2,1,0:T(8,128)(2,1)} %errors.1.refs_0_), channel_id=1, source_target_pairs={{0,6},{2,4},{4,2},{6,0},{8,14},{10,12},{12,10},{14,8},{1,7},{3,5},... | collective-permute-start | bytes 344072 | tf_op jit(solution)/shard_map/ppermute | solution.py:42
  56.9 6.0 %collective-permute-start.14 = (bf16[2,1,32,896]{3,2,1,0:T(8,128)(2,1)}, bf16[2,1,32,896]{3,2,1,0:T(8,128)(2,1)S(1)}, u32[]{:S(2)}, u32[]{:S(2)}) collective-permute-start(bf16[2,1,32,896]{3,2,1,0:T(8,128)(2,1)} %errors.1.refs_0_), channel_id=1, source_target_pairs={{0,4},{2,6},{4,0},{6,2},{8,12},{10,14},{12,8},{14,10},{1,5},{3,7},... | collective-permute-start | bytes 344072 | tf_op jit(solution)/shard_map/ppermute | solution.py:42
  58.7 5.0 %collective-permute-start.13 = (bf16[2,1,32,896]{3,2,1,0:T(8,128)(2,1)}, bf16[2,1,32,896]{3,2,1,0:T(8,128)(2,1)S(1)}, u32[]{:S(2)}, u32[]{:S(2)}) collective-permute-start(bf16[2,1,32,896]{3,2,1,0:T(8,128)(2,1)} %errors.1.refs_0_), channel_id=1, source_target_pairs={{0,2},{2,0},{4,6},{6,4},{8,10},{10,8},{12,14},{14,12},{1,3},{3,1},... | collective-permute-start | bytes 344072 | tf_op jit(solution)/shard_map/ppermute | solution.py:42
  62.4 1.3 %copy-start.13 = (bf16[2,1,32,896]{3,2,1,0:T(8,128)(2,1)}, bf16[2,1,32,896]{3,2,1,0:T(8,128)(2,1)S(1)}, u32[]{:S(2)}) copy-start(bf16[2,1,32,896]{3,2,1,0:T(8,128)(2,1)S(1)} %collective-permute-done.15.refs_3_) | copy-start | bytes 344068
  62.9 0.8 copy-start.15
  67.3 8.8 %copy-start.18 = (bf16[4,1,128,224]{3,2,1,0:T(8,128)(2,1)S(1)}, bf16[4,1,128,224]{3,2,1,0:T(8,128)(2,1)}, u32[]{:S(2)}) copy-start(bf16[4,1,128,224]{3,2,1,0:T(8,128)(2,1)} %get-tuple-element.16) | copy-start | bytes 688132
  67.3 3.8 %collective-permute-start.16 = (bf16[256,512]{1,0:T(8,128)(2,1)}, bf16[256,512]{1,0:T(8,128)(2,1)S(1)}, u32[]{:S(2)}, u32[]{:S(2)}) collective-permute-start(bf16[256,512]{1,0:T(8,128)(2,1)} %get-tuple-element.24), channel_id=1, source_target_pairs={{16,0},{17,1},{18,2},{19,3},{20,4},{21,5},{22,6},{23,7},{24,8},{25... | collective-permute-start | bytes 786440 | tf_op jit(solution)/shard_map/ppermute | solution.py:244
  71.1 0.7 copy-start.6
  74.6 14.2 %collective-permute-start.17 = (bf16[256,512]{1,0:T(8,128)(2,1)}, bf16[256,512]{1,0:T(8,128)(2,1)S(1)}, u32[]{:S(2)}, u32[]{:S(2)}) collective-permute-start(bf16[256,512]{1,0:T(8,128)(2,1)} %own_term.1.term), channel_id=1, source_target_pairs={{0,1},{1,0},{2,3},{3,2},{4,5},{5,4},{6,7},{7,6},{8,9},{9,8},{10,11... | collective-permute-start | bytes 786440 | tf_op jit(solution)/shard_map/ppermute | solution.py:46
  76.1 12.7 %collective-permute-start.4 = (bf16[4,1,128,224]{3,2,1,0:T(8,128)(2,1)S(1)}, bf16[4,1,128,224]{3,2,1,0:T(8,128)(2,1)S(1)}, u32[]{:S(2)}, u32[]{:S(2)}) collective-permute-start(bf16[4,1,128,224]{3,2,1,0:T(8,128)(2,1)S(1)} %copy-done.18), channel_id=1, source_target_pairs={{0,1},{1,0},{2,3},{3,2},{4,5},{5,4},{6,7},{7,6},{8,9},{9,8},{10,11... | collective-permute-start | bytes 688136 | tf_op jit(solution)/shard_map/ppermute | solution.py:46
  88.8 0.7 copy-start.5
  89.5 0.7 copy-start.4
  (5 other events, 3.3 us)
